TPU v7x, 32 devices: a whole 2x2x4 slice. The times are simulated.
32 devices in a mesh: grp: 2 (over y), pb: 4 (over z), re: 2 (over x), ka: 2 (over core).
Axes of the slice: x: 2, y: 2, z: 4, core: 2. Of those that a mesh axis runs over, the one named last changes fastest.
Arguments:
- g_wann: bfloat16 [2, 1024, 128, 256], P(None, 'pb', ('grp', 're'), 'ka'), parts along dimension 2, may hold values from -0.0234375 to 0.0234375
- phonon_phase: bfloat16 [2, 2048, 1024], P(None, 'pb'), may hold values from -1 to 1, as said below
- electron_phase: bfloat16 [2, 8, 64], replicated, may hold values from -1 to 1, as said below
Outputs:
- coupling: float32 [16, 2, 2048, 256], P(('grp', 're'), None, 'pb', 'ka'), parts along dimension 0
There are 2 independent parts, one for each index of `grp`. A program takes and returns all parts, laid end to end along the dimension named above; an argument that names none is the same for every part. Nothing has to cross between parts.
Inputs may be any that keep to these rules, and one draw needn't show every extreme that they name: `phonon_phase`: entries 0 and 1 along the first dimension are the cosine and sine of one angle. `electron_phase`: entries 0 and 1 along the first dimension are the cosine and sine of one angle.
All inputs are finite; a program needn't handle non-finite values.
Results may differ from a plain program's by a relative error of at most 0.0029.
Values may be sent and summed in bfloat16 or wider, within the bound.
A program may use at most 64 MiB of HBM per device.

v0:
```python
import jax
import jax.numpy as jnp
from jax import lax
from jax.sharding import PartitionSpec as P


def electron_term(phase, wann_real, wann_imag):
    real_part = jnp.einsum(
        "ke,peb->kpb", phase[0], wann_real, preferred_element_type=jnp.float32
    ) - jnp.einsum("ke,peb->kpb", phase[1], wann_imag, preferred_element_type=jnp.float32)
    imag_part = jnp.einsum(
        "ke,peb->kpb", phase[0], wann_imag, preferred_element_type=jnp.float32
    ) + jnp.einsum("ke,peb->kpb", phase[1], wann_real, preferred_element_type=jnp.float32)
    return jnp.stack([real_part, imag_part])


def body(g_wann, phonon_phase, electron_phase):
    local_vectors = g_wann.shape[2]
    offset = lax.axis_index("re") * local_vectors
    own_phase = lax.dynamic_slice_in_dim(electron_phase, offset, local_vectors, 2)
    partial_value = electron_term(own_phase, g_wann[0], g_wann[1])
    summed = lax.psum_scatter(partial_value, "re", scatter_dimension=1, tiled=True)
    bloch = summed.astype(jnp.bfloat16)
    cos_table = phonon_phase[0]
    sin_table = phonon_phase[1]
    piece = lax.all_gather(bloch, "pb", axis=2, tiled=True)
    acc_real = jnp.einsum(
        "qp,kpb->kqb", cos_table, piece[0], preferred_element_type=jnp.float32
    ) - jnp.einsum("qp,kpb->kqb", sin_table, piece[1], preferred_element_type=jnp.float32)
    acc_imag = jnp.einsum(
        "qp,kpb->kqb", cos_table, piece[1], preferred_element_type=jnp.float32
    ) + jnp.einsum("qp,kpb->kqb", sin_table, piece[0], preferred_element_type=jnp.float32)
    acc_real, acc_imag = (acc_real, acc_imag)
    return jnp.stack([acc_real, acc_imag], axis=1)


def solution(mesh):
    placed = (P(None, "pb", ("grp", "re"), "ka"), P(None, "pb", None), P())
    return jax.shard_map(
        body,
        mesh=mesh,
        in_specs=placed,
        out_specs=P(("grp", "re"), None, "pb", "ka"),
        check_vma=False,
    )
```

profile of v0, /device:TPU:0, one launch (start us, length us, event | category | flops | bytes accessed | tf_op | source)
XLA Modules:
  0.0 110.9 jit_solution(2155230755220057174)
XLA Ops:
  6.5 0.0 copy-start
  6.5 0.0 reduce-scatter.2.cloned.1.call-start
  6.5 0.7 copy-done
  7.2 0.0 copy-start.1
  7.2 2.2 %fusion = f32[8,256,128]{2,0,1:T(8,128)S(1)} fusion(bf16[2,256,32,128]{3,2,1,0:T(8,128)(2,1)} %param.3, bf16[2,8,64]{2,1,0:T(8,128)(2,1)S(1)} %copy-done, s32[]{:T(128)S(6)} %select_n.3), kind=kOutput, calls=%fused_computation.2 | convolution fusion | flops 16777216 | bytes 3147780 | tf_op jit(solution)/shard_map/ke,peb->kpb/dot_general | solution.py:11
  9.4 2.0 %fusion.2 = f32[8,256,128]{2,0,1:T(8,128)S(1)} fusion(bf16[2,256,32,128]{3,2,1,0:T(8,128)(2,1)} %param.3, bf16[2,8,64]{2,1,0:T(8,128)(2,1)S(1)} %copy-done, s32[]{:T(128)S(6)} %add.18, s32[]{:T(128)S(6)} %select_n.3), kind=kOutput, calls=%fused_computation.4 | convolution fusion | flops 16777216 | bytes 3147784 | tf_op jit(solution)/shard_map/ke,peb->kpb/dot_general | solution.py:10
  11.5 0.0 copy-done.1
  11.5 0.5 fusion.21
  11.9 0.5 fusion.15
  12.4 0.1 pad_maximum_fusion
  12.5 1.7 %copy.9 = f32[2,8,256,128]{3,2,0,1:T(8,128)} copy(f32[2,8,256,128]{3,1,2,0:T(8,128)S(1)} %pad_maximum_fusion) | data formatting | bytes 4194304 | tf_op jit(solution)/shard_map/stack | solution.py:14
  14.2 0.0 copy-start.2
  14.2 0.0 reduce-scatter.2.cloned.1.call-update
  14.3 0.0 all-gather.2.cloned.1.call-start
  14.3 34.7 %reduce-scatter.2.cloned.1.call-done = f32[2,4,256,128]{3,2,0,1:T(8,128)} async-done(((f32[2,8,256,128]{3,2,0,1:T(8,128)}), f32[2,4,256,128]{3,2,0,1:T(8,128)}) %reduce-scatter.2.cloned.1.call-update) | async-done | bytes 1048592 | tf_op jit(solution)/shard_map/reduce_scatter | solution.py:22
  49.0 2.2 %copy.10 = bf16[2,4,256,128]{2,3,1,0:T(8,128)(2,1)} copy(f32[2,4,256,128]{3,2,0,1:T(8,128)} %reduce-scatter.2.cloned.1.call-done) | data formatting | bytes 1572864 | tf_op jit(solution)/shard_map/reduce_scatter | solution.py:22
  51.3 0.0 all-gather.2.cloned.1.call-update
  51.3 46.4 %all-gather.2.cloned.1.call-done = bf16[2,4,1024,128]{2,3,1,0:T(8,128)(2,1)} async-done(((bf16[2,4,256,128]{2,3,1,0:T(8,128)(2,1)}), bf16[2,4,1024,128]{2,3,1,0:T(8,128)(2,1)}) %all-gather.2.cloned.1.call-update) | async-done | bytes 2097168 | tf_op jit(solution)/shard_map/all_gather | solution.py:26
  97.7 0.0 copy-done.2
  97.7 0.0 copy-start.3
  97.7 2.1 %fusion.28 = f32[4,128,512]{2,1,0:T(8,128)S(1)} fusion(bf16[2,4,1024,128]{2,3,1,0:T(8,128)(2,1)} %all-gather.2.cloned.1.call-done, bf16[2,512,1024]{2,1,0:T(8,128)(2,1)S(1)} %copy-done.2), kind=kOutput, calls=%fused_computation.26 | convolution fusion | flops 536870912 | bytes 3145728 | tf_op jit(solution)/shard_map/qp,kpb->kqb/dot_general | solution.py:30
  99.8 0.0 copy-done.3
  99.8 0.7 fusion.30
  100.6 0.7 fusion.24
  101.3 0.7 fusion.25
  102.1 0.2 pad_maximum_fusion.1
  102.3 1.8 %copy.11 = f32[4,2,512,128]{3,2,1,0:T(8,128)} copy(f32[4,2,512,128]{2,3,0,1:T(8,128)S(1)} %pad_maximum_fusion.1) | data formatting | bytes 4194304 | tf_op jit(solution)/shard_map/stack | solution.py:34
Async XLA Ops:
  6.5 0.7 copy-start
  6.5 42.5 %reduce-scatter.2.cloned.1.call-start = ((), (), s32[]{:S(2)}) async-start(), calls=%async_computation.1 | async-start | bytes 3145728 | tf_op jit(solution)/shard_map/reduce_scatter | solution.py:22
  7.2 4.2 %copy-start.1 = (bf16[2,256,32,128]{3,2,1,0:T(8,128)(2,1)S(1)}, bf16[2,256,32,128]{3,2,1,0:T(8,128)(2,1)}, u32[]{:S(2)}) copy-start(bf16[2,256,32,128]{3,2,1,0:T(8,128)(2,1)} %param.3) | copy-start | bytes 12582916
  14.2 83.5 %copy-start.2 = (bf16[2,512,1024]{2,1,0:T(8,128)(2,1)S(1)}, bf16[2,512,1024]{2,1,0:T(8,128)(2,1)}, u32[]{:S(2)}) copy-start(bf16[2,512,1024]{2,1,0:T(8,128)(2,1)} %param.4) | copy-start | bytes 6291460
  14.3 83.4 %all-gather.2.cloned.1.call-start = ((), (), s32[]{:S(2)}) async-start(), calls=%async_computation.2 | async-start | bytes 2621440 | tf_op jit(solution)/shard_map/all_gather | solution.py:26
  97.7 2.1 %copy-start.3 = (bf16[2,4,1024,128]{2,3,1,0:T(8,128)(2,1)S(1)}, bf16[2,4,1024,128]{2,3,1,0:T(8,128)(2,1)}, u32[]{:S(2)}) copy-start(bf16[2,4,1024,128]{2,3,1,0:T(8,128)(2,1)} %all-gather.2.cloned.1.call-done) | copy-start | bytes 6291460
Sparse Core Ops, SparseCore 0:
  14.4 34.6 reduce-scatter.1
  51.4 46.2 all-gather.1
where the time goes:
time: 111 us
  waiting for transfers between devices  81.2 us (73%)
  between operations  13.5 us (12%)
  matrix products  9.5 us (9%)
  local copies, waits for them, and re-layouts  6.43 us (6%)
    all_gather x1, waiting for transfers between devices, body(): piece = lax.all_gather(bloch, 'pb', axis=2, tiled=True)  46.4 us
    reduce_scatter x1, waiting for transfers between devices, body(): lax.psum_scatter(partial_value, 're', scatter_dimension=1, tiled=True)  34.7 us
    reduce_scatter x1, local copies, waits for them, and re-layouts, body(): lax.psum_scatter(partial_value, 're', scatter_dimension=1, tiled=True)  2.22 us
  transfers between devices with their start and end apart: 2, of which 2 were waited for; matrix products, arithmetic and copies ran while one was open for 0% of the time, Pallas kernels for 0%

commit v1 on v0

v1 whole, which is shorter than its diff:
```python
import functools
import jax
import jax.numpy as jnp
from jax import lax
from jax.experimental import pallas as pl
from jax.experimental.pallas import tpu as pltpu
from jax.sharding import PartitionSpec as P

MESH = pl.DeviceIdType.MESH
GROUP = 8
BF16 = jnp.bfloat16
F32 = jnp.float32


def iota(shape, dim):
    return lax.broadcasted_iota(jnp.int32, shape, dim)


def kernel(
    n_re, n_pb, halves,
    g_hbm, ph_hbm, el_ref, out_hbm,
    g, ph, el_block, part, x_recv, gath, out,
    g_sem, ph_sem, out_sem, x_send, x_got, z_send, z_got,
):
    x = lax.axis_index("re")
    z = lax.axis_index("pb")
    k_all, p_loc, width = part.shape
    b = width // 2
    k_own = k_all // n_re
    p_half = p_loc // halves
    e_all = el_ref.shape[2]
    e_loc = g.shape[1] // p_loc
    chunks = k_own * halves
    q_loc = ph.shape[1]

    def g_copy(h):
        rows = pl.ds(h * p_half * e_loc, p_half * e_loc)
        return pltpu.make_async_copy(g_hbm.at[:, rows, :], g.at[:, rows, :], g_sem.at[h])

    for h in range(halves):
        g_copy(h).start()
    ph_copy = pltpu.make_async_copy(ph_hbm, ph, ph_sem)
    ph_copy.start()

    barrier = pltpu.get_barrier_semaphore()
    for d in range(1, n_re):
        pl.semaphore_signal(barrier, inc=1, device_id={"re": lax.rem(x + d, n_re)}, device_id_type=MESH)

    @pl.when(z > 0)
    def _():
        pl.semaphore_signal(barrier, inc=1, device_id={"pb": z - 1}, device_id_type=MESH)

    @pl.when(z < n_pb - 1)
    def _():
        pl.semaphore_signal(barrier, inc=1, device_id={"pb": z + 1}, device_id_type=MESH)

    rows, cols = k_all * GROUP, GROUP * e_loc
    spread_k = (iota((rows, k_all), 0) // GROUP == iota((rows, k_all), 1)).astype(BF16)
    spread_e = (iota((e_all, cols), 0) == x * e_loc + iota((e_all, cols), 1) % e_loc).astype(BF16)
    same_p = iota((rows, cols), 0) % GROUP == iota((rows, cols), 1) // e_loc

    def spread(table):
        t = jnp.dot(spread_k, table, preferred_element_type=F32).astype(BF16)
        t = jnp.dot(t, spread_e, preferred_element_type=F32)
        return jnp.where(same_p, t, 0.0)

    cos_e = spread(el_ref[0])
    sin_e = spread(el_ref[1])
    el_block[0:rows, 0:cols] = cos_e.astype(BF16)
    el_block[0:rows, cols:] = (-sin_e).astype(BF16)
    el_block[rows:, 0:cols] = sin_e.astype(BF16)
    el_block[rows:, cols:] = cos_e.astype(BF16)

    n_meet = n_re - 1 + jnp.where(z > 0, 1, 0) + jnp.where(z < n_pb - 1, 1, 0)
    pl.semaphore_wait(barrier, n_meet)

    def x_copy(c, d):
        k, h = c // halves, c % halves
        there = pl.ds(pl.multiple_of(h * p_half, p_half), p_half)
        to = lax.rem(x + d, n_re)
        return pltpu.make_async_remote_copy(
            src_ref=part.at[to * k_own + k, there, :],
            dst_ref=x_recv.at[d - 1, k, there, :],
            send_sem=x_send.at[d - 1, c],
            recv_sem=x_got.at[d - 1, c],
            device_id={"re": to},
            device_id_type=MESH,
        )

    for h in range(halves):
        g_copy(h).wait()

        @pl.loop(h * (p_half // GROUP), (h + 1) * (p_half // GROUP), unroll=2)
        def _(j):
            at = pl.ds(pl.multiple_of(j * cols, cols), cols)
            both = jnp.concatenate([g[0, at, :], g[1, at, :]], axis=0)
            res = jnp.dot(el_block[...], both, preferred_element_type=F32)
            p_at = pl.ds(pl.multiple_of(j * GROUP, GROUP), GROUP)
            for c in range(2):
                for k in range(k_all):
                    first = (c * k_all + k) * GROUP
                    part[k, p_at, c * b:(c + 1) * b] = res[first:first + GROUP]

        for d in range(1, n_re):
            x_copy(h, d).start()
    for c in range(halves, chunks):
        for d in range(1, n_re):
            x_copy(c, d).start()

    def z_copy(c, source, way):
        k, h = c // halves, c % halves
        there = pl.ds(pl.multiple_of(source * p_loc + h * p_half, p_half), p_half)
        block = gath.at[k, there, :]
        return pltpu.make_async_remote_copy(
            src_ref=block,
            dst_ref=block,
            send_sem=z_send.at[way, c, source],
            recv_sem=z_got.at[c, source],
            device_id={"pb": z + 1 if way else z - 1},
            device_id_type=MESH,
        )

    @pl.loop(0, chunks + n_pb - 2)
    def _(t):
        @pl.when(t < chunks)
        def _():
            k, h = t // halves, t % halves
            there = pl.ds(pl.multiple_of(h * p_half, p_half), p_half)
            for d in range(1, n_re):
                x_copy(t, d).wait_recv()
            total = part[x * k_own + k, there, :]
            for d in range(1, n_re):
                total = total + x_recv[d - 1, k, there, :]
            mine = pl.ds(pl.multiple_of(z * p_loc + h * p_half, p_half), p_half)
            gath[k, mine, :] = total.astype(BF16)

            @pl.when(z > 0)
            def _():
                z_copy(t, z, 0).start()

            @pl.when(z < n_pb - 1)
            def _():
                z_copy(t, z, 1).start()

        for d in range(1, n_pb - 1):
            c = t - d
            ok = (c >= 0) & (c < chunks)

            @pl.when(ok & (z - d >= 0) & (z < n_pb - 1))
            def _():
                z_copy(c, z - d, 1).wait_recv()
                z_copy(c, z - d, 1).start()

            @pl.when(ok & (z + d < n_pb) & (z > 0))
            def _():
                z_copy(c, z + d, 0).wait_recv()
                z_copy(c, z + d, 0).start()

    ph_copy.wait()
    q_tile = min(256, q_loc)

    def out_copy(k):
        return pltpu.make_async_copy(out.at[k], out_hbm.at[k], out_sem.at[k])

    @pl.loop(0, k_own)
    def _(k):
        for h in range(halves):
            c = k * halves + h
            for s in range(n_pb):
                @pl.when(((s < z) & (z == n_pb - 1)) | ((s > z) & (z == 0)))
                def _():
                    z_copy(c, s, 0).wait_recv()

        @pl.loop(0, q_loc // q_tile)
        def _(i):
            at = pl.ds(pl.multiple_of(i * q_tile, q_tile), q_tile)
            data = gath[k]
            by_cos = jnp.dot(ph[0, at, :], data, preferred_element_type=F32)
            by_sin = jnp.dot(ph[1, at, :], data, preferred_element_type=F32)
            out[k, 0, at, :] = by_cos[:, :b] - by_sin[:, b:]
            out[k, 1, at, :] = by_cos[:, b:] + by_sin[:, :b]

        out_copy(k).start()

    @pl.loop(0, chunks)
    def _(c):
        for d in range(1, n_re):
            x_copy(c, d).wait_send()
        for s in range(n_pb):
            @pl.when((s >= z) & (z > 0))
            def _():
                z_copy(c, s, 0).wait_send()

            @pl.when((s <= z) & (z < n_pb - 1))
            def _():
                z_copy(c, s, 1).wait_send()

    for k in range(k_own):
        out_copy(k).wait()


def body(n_re, n_pb, g_wann, phonon_phase, electron_phase):
    _, p_loc, e_loc, b = g_wann.shape
    _, q_loc, p_all = phonon_phase.shape
    k_all = electron_phase.shape[1]
    k_own = k_all // n_re
    halves = 2
    chunks = k_own * halves
    g = g_wann.reshape(2, p_loc * e_loc, b)
    anywhere = pl.BlockSpec(memory_space=pl.ANY)
    return pl.pallas_call(
        functools.partial(kernel, n_re, n_pb, halves),
        out_shape=jax.ShapeDtypeStruct((k_own, 2, q_loc, b), F32),
        in_specs=[anywhere, anywhere, pl.BlockSpec(memory_space=pltpu.VMEM)],
        out_specs=anywhere,
        scratch_shapes=[
            pltpu.VMEM(g.shape, BF16),
            pltpu.VMEM(phonon_phase.shape, BF16),
            pltpu.VMEM((2 * k_all * GROUP, 2 * GROUP * e_loc), BF16),
            pltpu.VMEM((k_all, p_loc, 2 * b), F32),
            pltpu.VMEM((n_re - 1, k_own, p_loc, 2 * b), F32),
            pltpu.VMEM((k_own, p_all, 2 * b), BF16),
            pltpu.VMEM((k_own, 2, q_loc, b), F32),
            pltpu.SemaphoreType.DMA((halves,)),
            pltpu.SemaphoreType.DMA,
            pltpu.SemaphoreType.DMA((k_own,)),
            pltpu.SemaphoreType.DMA((n_re - 1, chunks)),
            pltpu.SemaphoreType.DMA((n_re - 1, chunks)),
            pltpu.SemaphoreType.DMA((2, chunks, n_pb)),
            pltpu.SemaphoreType.DMA((chunks, n_pb)),
        ],
        compiler_params=pltpu.CompilerParams(
            collective_id=0, has_side_effects=True, vmem_limit_bytes=60 * 1024 * 1024
        ),
    )(g, phonon_phase, electron_phase)


def solution(mesh):
    placed = (P(None, "pb", ("grp", "re"), "ka"), P(None, "pb", None), P())
    return jax.shard_map(
        functools.partial(body, mesh.shape["re"], mesh.shape["pb"]),
        mesh=mesh,
        in_specs=placed,
        out_specs=P(("grp", "re"), None, "pb", "ka"),
        check_vma=False,
    )
```

time: 111 us -> 54.2 us (0.49)
  waiting for transfers between devices: 81.2 us -> 0 us
  Pallas kernels: 0 us -> 50.9 us
  between operations: 13.5 us -> 0.01 us
  matrix products: 9.5 us -> 0 us
  local copies, waits for them, and re-layouts: 6.43 us -> 3.06 us
    pallas_call x0 -> x1, Pallas kernels: none -> 50.9 us  [body(): pl.pallas_call(functools.partial(kernel, n_re, n_pb, halves), out_shape=j...]
    all_gather x1 -> x0, waiting for transfers between devices: 46.4 us -> none  [body(): piece = lax.all_gather(bloch, 'pb', axis=2, tiled=True)]
    reduce_scatter x1 -> x0, waiting for transfers between devices: 34.7 us -> none  [body(): lax.psum_scatter(partial_value, 're', scatter_dimension=1, tiled=True)]
    dot_general x8 -> x0, matrix products: 9.5 us -> none  [the longest x1 2.19 us: electron_term(): jnp.einsum('ke,peb->kpb', phase[0], wann_imag, preferred_element_type=jnp...]
    another operation x2 -> x0, local copies, waits for them, and re-layouts: 3.51 us -> none  [the longest x1 1.81 us: body(): return jnp.stack([acc_real, acc_imag], axis=1)]
    unnamed x8 -> x1, local copies, waits for them, and re-layouts: 0.7 us -> 3.06 us
    reduce_scatter x1 -> x0, local copies, waits for them, and re-layouts: 2.22 us -> none  [body(): lax.psum_scatter(partial_value, 're', scatter_dimension=1, tiled=True)]
  transfers between devices with their start and end apart: 2 -> 0, of which waited for: 2 -> 0; matrix products, arithmetic and copies ran while one was open for 0% -> 0% of each run, Pallas kernels for 0% -> 0%
where the time goes in v1:
time: 54.2 us; the launch traced here: 54 us
  Pallas kernels  50.9 us (94%)
  local copies, waits for them, and re-layouts  3.06 us (6%)
    pallas_call x1, Pallas kernels, body(): pl.pallas_call(functools.partial(kernel, n_re, n_pb, halves), out_shape=j...  50.9 us
    unnamed x1, local copies, waits for them, and re-layouts  3.06 us

profile of v1, /device:TPU:0, one launch (start us, length us, event | category | flops | bytes accessed | tf_op | source)
XLA Modules:
  0.0 54.0 jit_solution(10819873622437470296)
XLA Ops:
  0.0 50.9 %shard_map.37 = f32[4,2,512,128]{3,2,1,0:T(8,128)} custom-call(bf16[2,8192,128]{2,1,0:T(8,128)(2,1)} %bitcast.1, bf16[2,512,1024]{2,1,0:T(8,128)(2,1)} %ph_hbm.1, bf16[2,8,64]{2,1,0:T(8,128)(2,1)} %el_ref.1), custom_call_target="tpu_custom_call" | custom-call | tf_op jit(solution)/shard_map/pallas_call | solution.py:211
  50.9 3.1 %copy.5 = f32[4,2,512,128]{3,2,1,0:T(8,128)} copy(f32[4,2,512,128]{3,2,1,0:T(8,128)} %shard_map.37) | data formatting | bytes 4194304

commit v2 on v1

--- a/solution.py
+++ b/solution.py
@@ -18,9 +18,9 @@
 
 def kernel(
     n_re, n_pb, halves,
-    g_hbm, ph_hbm, el_ref, out_hbm,
-    g, ph, el_block, part, x_recv, gath, out,
-    g_sem, ph_sem, out_sem, x_send, x_got, z_send, z_got,
+    g_hbm, ph_hbm, el_ref, out,
+    g, ph, el_block, part, x_first, x_first_recv, x_recv, gath,
+    g_sem, ph_sem, x_send, x_got, z_send, z_got,
 ):
     x = lax.axis_index("re")
     z = lax.axis_index("pb")
@@ -73,6 +73,18 @@
 
     n_meet = n_re - 1 + jnp.where(z > 0, 1, 0) + jnp.where(z < n_pb - 1, 1, 0)
     pl.semaphore_wait(barrier, n_meet)
+
+    def x_first_copy(h, d):
+        there = pl.ds(pl.multiple_of(h * p_half, p_half), p_half)
+        to = lax.rem(x + d, n_re)
+        return pltpu.make_async_remote_copy(
+            src_ref=x_first.at[to, there, :],
+            dst_ref=x_first_recv.at[d - 1, there, :],
+            send_sem=x_send.at[d - 1, h],
+            recv_sem=x_got.at[d - 1, h],
+            device_id={"re": to},
+            device_id_type=MESH,
+        )
 
     def x_copy(c, d):
         k, h = c // halves, c % halves
@@ -101,8 +113,11 @@
                     first = (c * k_all + k) * GROUP
                     part[k, p_at, c * b:(c + 1) * b] = res[first:first + GROUP]
 
+        there = pl.ds(h * p_half, p_half)
+        for r in range(n_re):
+            x_first[r, there, :] = part[r * k_own, there, :].astype(BF16)
         for d in range(1, n_re):
-            x_copy(h, d).start()
+            x_first_copy(h, d).start()
     for c in range(halves, chunks):
         for d in range(1, n_re):
             x_copy(c, d).start()
@@ -126,13 +141,23 @@
         def _():
             k, h = t // halves, t % halves
             there = pl.ds(pl.multiple_of(h * p_half, p_half), p_half)
-            for d in range(1, n_re):
-                x_copy(t, d).wait_recv()
-            total = part[x * k_own + k, there, :]
-            for d in range(1, n_re):
-                total = total + x_recv[d - 1, k, there, :]
             mine = pl.ds(pl.multiple_of(z * p_loc + h * p_half, p_half), p_half)
-            gath[k, mine, :] = total.astype(BF16)
+
+            @pl.when(t < halves)
+            def _():
+                total = part[x * k_own, there, :]
+                for d in range(1, n_re):
+                    x_first_copy(t, d).wait_recv()
+                    total = total + x_first_recv[d - 1, there, :].astype(F32)
+                gath[0, mine, :] = total.astype(BF16)
+
+            @pl.when(t >= halves)
+            def _():
+                total = part[x * k_own + k, there, :]
+                for d in range(1, n_re):
+                    x_copy(t, d).wait_recv()
+                    total = total + x_recv[d - 1, k, there, :]
+                gath[k, mine, :] = total.astype(BF16)
 
             @pl.when(z > 0)
             def _():
@@ -158,9 +183,6 @@
 
     ph_copy.wait()
     q_tile = min(256, q_loc)
-
-    def out_copy(k):
-        return pltpu.make_async_copy(out.at[k], out_hbm.at[k], out_sem.at[k])
 
     @pl.loop(0, k_own)
     def _(k):
@@ -180,12 +202,16 @@
             out[k, 0, at, :] = by_cos[:, :b] - by_sin[:, b:]
             out[k, 1, at, :] = by_cos[:, b:] + by_sin[:, :b]
 
-        out_copy(k).start()
-
     @pl.loop(0, chunks)
     def _(c):
         for d in range(1, n_re):
-            x_copy(c, d).wait_send()
+            @pl.when(c < halves)
+            def _():
+                x_first_copy(c, d).wait_send()
+
+            @pl.when(c >= halves)
+            def _():
+                x_copy(c, d).wait_send()
         for s in range(n_pb):
             @pl.when((s >= z) & (z > 0))
             def _():
@@ -194,9 +220,6 @@
             @pl.when((s <= z) & (z < n_pb - 1))
             def _():
                 z_copy(c, s, 1).wait_send()
-
-    for k in range(k_own):
-        out_copy(k).wait()
 
 
 def body(n_re, n_pb, g_wann, phonon_phase, electron_phase):
@@ -204,35 +227,36 @@
     _, q_loc, p_all = phonon_phase.shape
     k_all = electron_phase.shape[1]
     k_own = k_all // n_re
-    halves = 2
+    halves = 4
     chunks = k_own * halves
     g = g_wann.reshape(2, p_loc * e_loc, b)
-    anywhere = pl.BlockSpec(memory_space=pl.ANY)
+    far = pl.BlockSpec(memory_space=pltpu.HBM)
+    near = pl.BlockSpec(memory_space=pltpu.VMEM)
     return pl.pallas_call(
         functools.partial(kernel, n_re, n_pb, halves),
         out_shape=jax.ShapeDtypeStruct((k_own, 2, q_loc, b), F32),
-        in_specs=[anywhere, anywhere, pl.BlockSpec(memory_space=pltpu.VMEM)],
-        out_specs=anywhere,
+        in_specs=[far, far, near],
+        out_specs=near,
         scratch_shapes=[
             pltpu.VMEM(g.shape, BF16),
             pltpu.VMEM(phonon_phase.shape, BF16),
             pltpu.VMEM((2 * k_all * GROUP, 2 * GROUP * e_loc), BF16),
             pltpu.VMEM((k_all, p_loc, 2 * b), F32),
+            pltpu.VMEM((n_re, p_loc, 2 * b), BF16),
+            pltpu.VMEM((n_re - 1, p_loc, 2 * b), BF16),
             pltpu.VMEM((n_re - 1, k_own, p_loc, 2 * b), F32),
             pltpu.VMEM((k_own, p_all, 2 * b), BF16),
-            pltpu.VMEM((k_own, 2, q_loc, b), F32),
             pltpu.SemaphoreType.DMA((halves,)),
             pltpu.SemaphoreType.DMA,
-            pltpu.SemaphoreType.DMA((k_own,)),
             pltpu.SemaphoreType.DMA((n_re - 1, chunks)),
             pltpu.SemaphoreType.DMA((n_re - 1, chunks)),
             pltpu.SemaphoreType.DMA((2, chunks, n_pb)),
             pltpu.SemaphoreType.DMA((chunks, n_pb)),
         ],
         compiler_params=pltpu.CompilerParams(
-            collective_id=0, has_side_effects=True, vmem_limit_bytes=60 * 1024 * 1024
+            collective_id=0, has_side_effects=True, vmem_limit_bytes=24 * 1024 * 1024
         ),
-    )(g, phonon_phase, electron_phase)
+    )(*(pltpu.with_memory_space_constraint(a, pltpu.HBM) for a in (g, phonon_phase, electron_phase)))
 
 
 def solution(mesh):

time: 54.2 us -> 53 us (0.978)
  local copies, waits for them, and re-layouts: 3.06 us -> 1.32 us
    unnamed x1, local copies, waits for them, and re-layouts: 3.06 us -> 1.32 us
where the time goes in v2:
time: 53 us; the launch traced here: 52.8 us
  Pallas kernels  51.4 us (97%)
  local copies, waits for them, and re-layouts  1.32 us (2%)
    pallas_call x1, Pallas kernels, body(): pl.pallas_call(functools.partial(kernel, n_re, n_pb, halves), out_shape=j...  51.4 us
    unnamed x1, local copies, waits for them, and re-layouts  1.32 us

profile of v2, /device:TPU:0, one launch (start us, length us, event | category | flops | bytes accessed | tf_op | source)
XLA Modules:
  0.0 52.8 jit_solution(14040043977557932387)
XLA Ops:
  0.0 51.4 %shard_map.37 = f32[4,2,512,128]{3,2,1,0:T(8,128)S(1)} custom-call(bf16[2,8192,128]{2,1,0:T(8,128)(2,1)} %bitcast.1, bf16[2,512,1024]{2,1,0:T(8,128)(2,1)} %ph_hbm.1, bf16[2,8,64]{2,1,0:T(8,128)(2,1)} %el_ref.1), custom_call_target="tpu_custom_call" | custom-call | tf_op jit(solution)/shard_map/pallas_call | solution.py:235
  51.5 1.3 %copy.5 = f32[4,2,512,128]{3,2,1,0:T(8,128)} copy(f32[4,2,512,128]{3,2,1,0:T(8,128)S(1)} %shard_map.37) | data formatting | bytes 4194304

commit v3 on v2

--- a/solution.py
+++ b/solution.py
@@ -8,6 +8,8 @@
 
 MESH = pl.DeviceIdType.MESH
 GROUP = 8
+PAIR = 2
+SLACK = 2
 BF16 = jnp.bfloat16
 F32 = jnp.float32
 
@@ -39,8 +41,6 @@
 
     for h in range(halves):
         g_copy(h).start()
-    ph_copy = pltpu.make_async_copy(ph_hbm, ph, ph_sem)
-    ph_copy.start()
 
     barrier = pltpu.get_barrier_semaphore()
     for d in range(1, n_re):
@@ -70,9 +70,6 @@
     el_block[0:rows, cols:] = (-sin_e).astype(BF16)
     el_block[rows:, 0:cols] = sin_e.astype(BF16)
     el_block[rows:, cols:] = cos_e.astype(BF16)
-
-    n_meet = n_re - 1 + jnp.where(z > 0, 1, 0) + jnp.where(z < n_pb - 1, 1, 0)
-    pl.semaphore_wait(barrier, n_meet)
 
     def x_first_copy(h, d):
         there = pl.ds(pl.multiple_of(h * p_half, p_half), p_half)
@@ -102,17 +99,24 @@
     for h in range(halves):
         g_copy(h).wait()
 
-        @pl.loop(h * (p_half // GROUP), (h + 1) * (p_half // GROUP), unroll=2)
+        @pl.loop(h * (p_half // GROUP // PAIR), (h + 1) * (p_half // GROUP // PAIR), unroll=2)
         def _(j):
-            at = pl.ds(pl.multiple_of(j * cols, cols), cols)
-            both = jnp.concatenate([g[0, at, :], g[1, at, :]], axis=0)
+            sides = []
+            for side in range(PAIR):
+                at = pl.ds(pl.multiple_of((j * PAIR + side) * cols, cols), cols)
+                sides.append(jnp.concatenate([g[0, at, :], g[1, at, :]], axis=0))
+            both = jnp.concatenate(sides, axis=1)
             res = jnp.dot(el_block[...], both, preferred_element_type=F32)
-            p_at = pl.ds(pl.multiple_of(j * GROUP, GROUP), GROUP)
-            for c in range(2):
-                for k in range(k_all):
-                    first = (c * k_all + k) * GROUP
-                    part[k, p_at, c * b:(c + 1) * b] = res[first:first + GROUP]
-
+            for side in range(PAIR):
+                p_at = pl.ds(pl.multiple_of((j * PAIR + side) * GROUP, GROUP), GROUP)
+                for c in range(2):
+                    for k in range(k_all):
+                        first = (c * k_all + k) * GROUP
+                        part[k, p_at, c * b:(c + 1) * b] = res[first:first + GROUP, side * b:(side + 1) * b]
+
+        if h == 0:
+            n_meet = n_re - 1 + jnp.where(z > 0, 1, 0) + jnp.where(z < n_pb - 1, 1, 0)
+            pl.semaphore_wait(barrier, n_meet)
         there = pl.ds(h * p_half, p_half)
         for r in range(n_re):
             x_first[r, there, :] = part[r * k_own, there, :].astype(BF16)
@@ -121,6 +125,8 @@
     for c in range(halves, chunks):
         for d in range(1, n_re):
             x_copy(c, d).start()
+    ph_copy = pltpu.make_async_copy(ph_hbm, ph, ph_sem)
+    ph_copy.start()
 
     def z_copy(c, source, way):
         k, h = c // halves, c % halves
@@ -135,7 +141,7 @@
             device_id_type=MESH,
         )
 
-    @pl.loop(0, chunks + n_pb - 2)
+    @pl.loop(0, chunks + (n_pb - 2) * (1 + SLACK))
     def _(t):
         @pl.when(t < chunks)
         def _():
@@ -168,7 +174,7 @@
                 z_copy(t, z, 1).start()
 
         for d in range(1, n_pb - 1):
-            c = t - d
+            c = t - d * (1 + SLACK)
             ok = (c >= 0) & (c < chunks)
 
             @pl.when(ok & (z - d >= 0) & (z < n_pb - 1))

time: 53 us -> 48.4 us (0.913)
  Pallas kernels: 51.4 us -> 46.9 us
    pallas_call x1, Pallas kernels: 51.4 us -> 46.9 us  [body(): pl.pallas_call(functools.partial(kernel, n_re, n_pb, halves), out_shape=j...]
where the time goes in v3:
time: 48.4 us; the launch traced here: 48.2 us
  Pallas kernels  46.9 us (97%)
  local copies, waits for them, and re-layouts  1.32 us (3%)
    pallas_call x1, Pallas kernels, body(): pl.pallas_call(functools.partial(kernel, n_re, n_pb, halves), out_shape=j...  46.9 us
    unnamed x1, local copies, waits for them, and re-layouts  1.32 us

profile of v3, /device:TPU:0, one launch (start us, length us, event | category | flops | bytes accessed | tf_op | source)
XLA Modules:
  0.0 48.2 jit_solution(8369184558992650999)
XLA Ops:
  0.0 46.9 %shard_map.37 = f32[4,2,512,128]{3,2,1,0:T(8,128)S(1)} custom-call(bf16[2,8192,128]{2,1,0:T(8,128)(2,1)} %bitcast.1, bf16[2,512,1024]{2,1,0:T(8,128)(2,1)} %ph_hbm.1, bf16[2,8,64]{2,1,0:T(8,128)(2,1)} %el_ref.1), custom_call_target="tpu_custom_call" | custom-call | tf_op jit(solution)/shard_map/pallas_call | solution.py:241
  46.9 1.3 %copy.5 = f32[4,2,512,128]{3,2,1,0:T(8,128)} copy(f32[4,2,512,128]{3,2,1,0:T(8,128)S(1)} %shard_map.37) | data formatting | bytes 4194304

commit v4 on v3

--- a/solution.py
+++ b/solution.py
@@ -9,7 +9,9 @@
 MESH = pl.DeviceIdType.MESH
 GROUP = 8
 PAIR = 2
-SLACK = 2
+UNROLL = 4
+AHEAD = 1
+SLACK = 0
 BF16 = jnp.bfloat16
 F32 = jnp.float32
 
@@ -20,9 +22,9 @@
 
 def kernel(
     n_re, n_pb, halves,
-    g_hbm, ph_hbm, el_ref, out,
-    g, ph, el_block, part, x_first, x_first_recv, x_recv, gath,
-    g_sem, ph_sem, x_send, x_got, z_send, z_got,
+    g_hbm, ph_hbm, el_hbm, out,
+    g, ph, el_ref, el_block, part, x_first, x_first_recv, x_recv, gath,
+    g_sem, ph_sem, el_sem, x_send, x_got, z_send, z_got,
 ):
     x = lax.axis_index("re")
     z = lax.axis_index("pb")
@@ -39,9 +41,6 @@
         rows = pl.ds(h * p_half * e_loc, p_half * e_loc)
         return pltpu.make_async_copy(g_hbm.at[:, rows, :], g.at[:, rows, :], g_sem.at[h])
 
-    for h in range(halves):
-        g_copy(h).start()
-
     barrier = pltpu.get_barrier_semaphore()
     for d in range(1, n_re):
         pl.semaphore_signal(barrier, inc=1, device_id={"re": lax.rem(x + d, n_re)}, device_id_type=MESH)
@@ -53,6 +52,11 @@
     @pl.when(z < n_pb - 1)
     def _():
         pl.semaphore_signal(barrier, inc=1, device_id={"pb": z + 1}, device_id_type=MESH)
+
+    el_copy = pltpu.make_async_copy(el_hbm, el_ref, el_sem)
+    el_copy.start()
+    for h in range(halves):
+        g_copy(h).start()
 
     rows, cols = k_all * GROUP, GROUP * e_loc
     spread_k = (iota((rows, k_all), 0) // GROUP == iota((rows, k_all), 1)).astype(BF16)
@@ -64,6 +68,7 @@
         t = jnp.dot(t, spread_e, preferred_element_type=F32)
         return jnp.where(same_p, t, 0.0)
 
+    el_copy.wait()
     cos_e = spread(el_ref[0])
     sin_e = spread(el_ref[1])
     el_block[0:rows, 0:cols] = cos_e.astype(BF16)
@@ -96,10 +101,52 @@
             device_id_type=MESH,
         )
 
+    def z_copy(c, source, way):
+        k, h = c // halves, c % halves
+        there = pl.ds(pl.multiple_of(source * p_loc + h * p_half, p_half), p_half)
+        block = gath.at[k, there, :]
+        return pltpu.make_async_remote_copy(
+            src_ref=block,
+            dst_ref=block,
+            send_sem=z_send.at[way, c, source],
+            recv_sem=z_got.at[c, source],
+            device_id={"pb": z + 1 if way else z - 1},
+            device_id_type=MESH,
+        )
+
+    def own_step(t):
+        k, h = t // halves, t % halves
+        there = pl.ds(pl.multiple_of(h * p_half, p_half), p_half)
+        mine = pl.ds(pl.multiple_of(z * p_loc + h * p_half, p_half), p_half)
+
+        @pl.when(t < halves)
+        def _():
+            total = part[x * k_own, there, :]
+            for d in range(1, n_re):
+                x_first_copy(t, d).wait_recv()
+                total = total + x_first_recv[d - 1, there, :].astype(F32)
+            gath[0, mine, :] = total.astype(BF16)
+
+        @pl.when(t >= halves)
+        def _():
+            total = part[x * k_own + k, there, :]
+            for d in range(1, n_re):
+                x_copy(t, d).wait_recv()
+                total = total + x_recv[d - 1, k, there, :]
+            gath[k, mine, :] = total.astype(BF16)
+
+        @pl.when(z > 0)
+        def _():
+            z_copy(t, z, 0).start()
+
+        @pl.when(z < n_pb - 1)
+        def _():
+            z_copy(t, z, 1).start()
+
     for h in range(halves):
         g_copy(h).wait()
 
-        @pl.loop(h * (p_half // GROUP // PAIR), (h + 1) * (p_half // GROUP // PAIR), unroll=2)
+        @pl.loop(h * (p_half // GROUP // PAIR), (h + 1) * (p_half // GROUP // PAIR), unroll=UNROLL)
         def _(j):
             sides = []
             for side in range(PAIR):
@@ -122,56 +169,19 @@
             x_first[r, there, :] = part[r * k_own, there, :].astype(BF16)
         for d in range(1, n_re):
             x_first_copy(h, d).start()
+        if h >= halves - AHEAD:
+            own_step(h - (halves - AHEAD))
     for c in range(halves, chunks):
         for d in range(1, n_re):
             x_copy(c, d).start()
     ph_copy = pltpu.make_async_copy(ph_hbm, ph, ph_sem)
     ph_copy.start()
 
-    def z_copy(c, source, way):
-        k, h = c // halves, c % halves
-        there = pl.ds(pl.multiple_of(source * p_loc + h * p_half, p_half), p_half)
-        block = gath.at[k, there, :]
-        return pltpu.make_async_remote_copy(
-            src_ref=block,
-            dst_ref=block,
-            send_sem=z_send.at[way, c, source],
-            recv_sem=z_got.at[c, source],
-            device_id={"pb": z + 1 if way else z - 1},
-            device_id_type=MESH,
-        )
-
-    @pl.loop(0, chunks + (n_pb - 2) * (1 + SLACK))
+    @pl.loop(AHEAD, chunks + (n_pb - 2) * (1 + SLACK))
     def _(t):
         @pl.when(t < chunks)
         def _():
-            k, h = t // halves, t % halves
-            there = pl.ds(pl.multiple_of(h * p_half, p_half), p_half)
-            mine = pl.ds(pl.multiple_of(z * p_loc + h * p_half, p_half), p_half)
-
-            @pl.when(t < halves)
-            def _():
-                total = part[x * k_own, there, :]
-                for d in range(1, n_re):
-                    x_first_copy(t, d).wait_recv()
-                    total = total + x_first_recv[d - 1, there, :].astype(F32)
-                gath[0, mine, :] = total.astype(BF16)
-
-            @pl.when(t >= halves)
-            def _():
-                total = part[x * k_own + k, there, :]
-                for d in range(1, n_re):
-                    x_copy(t, d).wait_recv()
-                    total = total + x_recv[d - 1, k, there, :]
-                gath[k, mine, :] = total.astype(BF16)
-
-            @pl.when(z > 0)
-            def _():
-                z_copy(t, z, 0).start()
-
-            @pl.when(z < n_pb - 1)
-            def _():
-                z_copy(t, z, 1).start()
+            own_step(t)
 
         for d in range(1, n_pb - 1):
             c = t - d * (1 + SLACK)
@@ -233,7 +243,7 @@
     _, q_loc, p_all = phonon_phase.shape
     k_all = electron_phase.shape[1]
     k_own = k_all // n_re
-    halves = 4
+    halves = 2
     chunks = k_own * halves
     g = g_wann.reshape(2, p_loc * e_loc, b)
     far = pl.BlockSpec(memory_space=pltpu.HBM)
@@ -241,11 +251,12 @@
     return pl.pallas_call(
         functools.partial(kernel, n_re, n_pb, halves),
         out_shape=jax.ShapeDtypeStruct((k_own, 2, q_loc, b), F32),
-        in_specs=[far, far, near],
+        in_specs=[far, far, far],
         out_specs=near,
         scratch_shapes=[
             pltpu.VMEM(g.shape, BF16),
             pltpu.VMEM(phonon_phase.shape, BF16),
+            pltpu.VMEM(electron_phase.shape, BF16),
             pltpu.VMEM((2 * k_all * GROUP, 2 * GROUP * e_loc), BF16),
             pltpu.VMEM((k_all, p_loc, 2 * b), F32),
             pltpu.VMEM((n_re, p_loc, 2 * b), BF16),
@@ -253,6 +264,7 @@
             pltpu.VMEM((n_re - 1, k_own, p_loc, 2 * b), F32),
             pltpu.VMEM((k_own, p_all, 2 * b), BF16),
             pltpu.SemaphoreType.DMA((halves,)),
+            pltpu.SemaphoreType.DMA,
             pltpu.SemaphoreType.DMA,
             pltpu.SemaphoreType.DMA((n_re - 1, chunks)),
             pltpu.SemaphoreType.DMA((n_re - 1, chunks)),

time: 48.4 us -> 47.4 us (0.979)
  Pallas kernels: 46.9 us -> 46 us
    pallas_call x1, Pallas kernels: 46.9 us -> 46 us  [body(): pl.pallas_call(functools.partial(kernel, n_re, n_pb, halves), out_shape=j...]
where the time goes in v4:
time: 47.4 us; the launch traced here: 47.3 us
  Pallas kernels  46 us (97%)
  local copies, waits for them, and re-layouts  1.32 us (3%)
    pallas_call x1, Pallas kernels, body(): pl.pallas_call(functools.partial(kernel, n_re, n_pb, halves), out_shape=j...  46 us
    unnamed x1, local copies, waits for them, and re-layouts  1.32 us

profile of v4, /device:TPU:0, one launch (start us, length us, event | category | flops | bytes accessed | tf_op | source)
XLA Modules:
  0.0 47.3 jit_solution(1503063652864055776)
XLA Ops:
  0.0 46.0 %shard_map.37 = f32[4,2,512,128]{3,2,1,0:T(8,128)S(1)} custom-call(bf16[2,8192,128]{2,1,0:T(8,128)(2,1)} %bitcast.1, bf16[2,512,1024]{2,1,0:T(8,128)(2,1)} %ph_hbm.1, bf16[2,8,64]{2,1,0:T(8,128)(2,1)} %el_hbm.1), custom_call_target="tpu_custom_call" | custom-call | tf_op jit(solution)/shard_map/pallas_call | solution.py:251
  46.0 1.3 %copy.5 = f32[4,2,512,128]{3,2,1,0:T(8,128)} copy(f32[4,2,512,128]{3,2,1,0:T(8,128)S(1)} %shard_map.37) | data formatting | bytes 4194304
